TPU v7x, 32 devices: a whole 2x2x4 slice. The times are simulated.
32 devices in a mesh: src: 4 (over x, core), rcv: 8 (over z, y).
Axes of the slice: x: 2, y: 2, z: 4, core: 2. Of those that a mesh axis runs over, the one named last changes fastest.
Arguments:
- wavefield: bfloat16 [1024, 1024, 256], P('src', 'rcv'), may hold values from -6 to 6
- inverse_wavelet: float32 [2, 64], replicated, may hold values from -0.05 to 0.05
Outputs:
- primaries: bfloat16 [1024, 1024, 256], P('src', 'rcv')
All inputs are finite; a program needn't handle non-finite values.
Results may differ from a plain program's by a relative error of at most 0.0091.
Values may be sent and summed in bfloat16 or wider, within the bound.
No kernel may reach another device: no remote copies, remote signals or barrier semaphores. Data moves between devices by JAX's collectives and lax.ppermute only.
A program may use at most 256 MiB of HBM per device.

v0:
```python
import math
import jax
import jax.numpy as jnp
from jax import lax
from jax.sharding import PartitionSpec as P

F0 = 8


def tables(count_t, count_f, first):
    times = jnp.arange(count_t, dtype=jnp.int32)
    freqs = first + jnp.arange(count_f, dtype=jnp.int32)
    phase = freqs[:, None] * times[None, :] % count_t
    angle = phase.astype(jnp.float32) * (2.0 * math.pi / count_t)
    rows = jnp.stack([jnp.cos(angle), -jnp.sin(angle)], 1).reshape(2 * count_f, count_t)
    forward = (rows / math.sqrt(count_t)).astype(jnp.bfloat16)
    inverse = (rows / math.sqrt(count_f)).astype(jnp.bfloat16)
    return (forward, inverse)


def combine(mirror_real, mirror_imag, sq_real, sq_imag, cube_real, cube_imag, wave_real, wave_imag):
    two_real = wave_real * wave_real - wave_imag * wave_imag
    two_imag = 2.0 * wave_real * wave_imag
    out_real = (
        mirror_real
        - (wave_real * sq_real - wave_imag * sq_imag)
        + (two_real * cube_real - two_imag * cube_imag)
    )
    out_imag = (
        mirror_imag
        - (wave_real * sq_imag + wave_imag * sq_real)
        + (two_real * cube_imag + two_imag * cube_real)
    )
    return (out_real, out_imag)


def multiply(left_side, right_side):
    return jnp.einsum("fmk,fkn->fmn", left_side, right_side, preferred_element_type=jnp.float32)


def complex_product(left_side, right_side):
    real_part = multiply(left_side[:, 0], right_side[:, 0]) - multiply(
        left_side[:, 1], right_side[:, 1]
    )
    imag_part = multiply(left_side[:, 0], right_side[:, 1]) + multiply(
        left_side[:, 1], right_side[:, 0]
    )
    return (real_part, imag_part)


def local(wavefield, inverse_wavelet):
    src_rows, rcv_cols, samples = wavefield.shape
    count_f = inverse_wavelet.shape[1]
    groups = lax.axis_size("rcv")
    per_dev = count_f // groups
    forward, inverse = tables(samples, count_f, F0)
    spectra = jnp.einsum(
        "ct,srt->csr", forward, wavefield, preferred_element_type=jnp.float32
    ).astype(jnp.bfloat16)
    spectra = spectra.reshape(groups, 2 * per_dev, src_rows, rcv_cols)
    slices = lax.all_to_all(spectra, "rcv", split_axis=0, concat_axis=3, tiled=True)
    total_cols = slices.shape[3]
    slices = slices.reshape(per_dev, 2, src_rows, total_cols)
    whole = lax.all_gather(slices, "src", axis=2, tiled=True).astype(jnp.float32)
    all_rows = (0.5 * (whole + jnp.swapaxes(whole, 2, 3))).astype(jnp.bfloat16)
    mirrored = lax.dynamic_slice_in_dim(all_rows, lax.axis_index("src") * src_rows, src_rows, 2)
    sq_real, sq_imag = complex_product(mirrored, all_rows)
    squared = jnp.stack([sq_real, sq_imag], 1).astype(jnp.bfloat16)
    cube_real, cube_imag = complex_product(squared, all_rows)
    wavelet = lax.dynamic_slice_in_dim(inverse_wavelet, lax.axis_index("rcv") * per_dev, per_dev, 1)
    wave_real = wavelet[0][:, None, None]
    wave_imag = wavelet[1][:, None, None]
    out_real, out_imag = combine(
        mirrored[:, 0].astype(jnp.float32),
        mirrored[:, 1].astype(jnp.float32),
        sq_real,
        sq_imag,
        cube_real,
        cube_imag,
        wave_real,
        wave_imag,
    )
    cleaned = (
        jnp.stack([out_real, out_imag], 1)
        .astype(jnp.bfloat16)
        .reshape(1, 2 * per_dev, src_rows, total_cols)
    )
    returned = lax.all_to_all(cleaned, "rcv", split_axis=3, concat_axis=0, tiled=True)
    returned = returned.reshape(2 * count_f, src_rows, rcv_cols)
    return jnp.einsum("csr,ct->srt", returned, inverse, preferred_element_type=jnp.float32).astype(
        jnp.bfloat16
    )


def solution(mesh):
    placed = (P("src", "rcv", None), P())
    return jax.shard_map(
        local, mesh=mesh, in_specs=placed, out_specs=P("src", "rcv", None), check_vma=False
    )
```

profile of v0, /device:TPU:0, one launch (start us, length us, event | category | flops | bytes accessed | tf_op | source)
XLA Modules:
  0.0 942.9 jit_solution(6739649526145548966)
XLA Ops:
  6.5 0.3 fusion.25
  6.9 0.6 multiply_convert_fusion.1
  7.5 0.1 copy.29
  7.6 11.1 %convolution_convert_fusion.1 = bf16[128,256,128]{2,0,1:T(8,128)(2,1)} fusion(bf16[128,256,1]{1,0,2:T(8,128)(2,1)S(1)} %reshape.171, bf16[256,128,256]{2,1,0:T(8,128)(2,1)} %param.2), kind=kOutput, calls=%fused_computation.18 | convolution fusion | flops 2151677952 | bytes 25231360 | tf_op jit(solution)/shard_map/ct,srt->csr/dot_general | solution.py:57
  18.8 13.0 %copy.30 = bf16[8,16,256,128]{2,3,1,0:T(8,128)(2,1)} copy(bf16[8,16,256,128]{3,1,0,2:T(8,128)(2,1)} %bitcast.70) | data formatting | bytes 16777216 | tf_op jit(solution)/shard_map/reshape | solution.py:60
  31.7 190.4 %all_to_all.30 = bf16[8,16,256,128]{2,3,1,0:T(8,128)(2,1)} all-to-all(bf16[8,16,256,128]{2,3,1,0:T(8,128)(2,1)} %copy.30), channel_id=1, replica_groups=mesh['src'=4,'rcv'=8] {'rcv'}, dimensions={0} | all-to-all | bytes 16777216 | tf_op jit(solution)/shard_map/all_to_all | solution.py:61
  222.2 7.9 copy.31
  230.1 7.4 copy.32
  237.4 0.0 all-gather.2.cloned.1.call-update
  237.4 0.1 constant_dynamic-slice_fusion
  237.5 0.5 multiply_subtract_fusion
  238.1 0.6 slice_bitcast_fusion.15
  238.7 204.0 %all-gather.2.cloned.1.call-done = bf16[8,2,1024,1024]{2,3,0,1:T(8,128)(2,1)} async-done(((bf16[8,2,256,1024]{2,3,0,1:T(8,128)(2,1)}), bf16[8,2,1024,1024]{2,3,0,1:T(8,128)(2,1)}) %all-gather.2.cloned.1.call-update) | async-done | bytes 33554448 | tf_op jit(solution)/shard_map/all_gather | solution.py:64
  442.7 46.2 %copy.33 = f32[8,2,1024,1024]{3,2,0,1:T(8,128)} copy(bf16[8,2,1024,1024]{2,3,0,1:T(8,128)(2,1)} %all-gather.2.cloned.1.call-done) | data formatting | bytes 100663296 | tf_op jit(solution)/shard_map/convert_element_type | solution.py:64
  488.9 42.8 %fusion.1 = bf16[8,2,1024,1024]{3,2,0,1:T(8,128)(2,1)} fusion(f32[8,2,1024,1024]{3,2,0,1:T(8,128)} %copy.33, bf16[8,2,1024,1024]{2,3,0,1:T(8,128)(2,1)} %all-gather.2.cloned.1.call-done), kind=kLoop, calls=%fused_computation.2 | loop fusion | flops 67108864 | bytes 134217728 | tf_op jit(solution)/shard_map/convert_element_type | solution.py:65
  531.7 14.8 %fusion.5 = f32[8,256,1024]{2,1,0:T(8,128)} fusion(bf16[8,2,1024,1024]{3,2,0,1:T(8,128)(2,1)} %fusion.1, s32[]{:T(128)S(6)} %select_n.27), kind=kOutput, calls=%fused_computation.8 | convolution fusion | flops 4294967296 | bytes 29360132 | tf_op jit(solution)/shard_map/fmk,fkn->fmn/dot_general | solution.py:38
  546.5 15.0 %fusion.4 = f32[8,256,1024]{2,1,0:T(8,128)} fusion(bf16[8,2,1024,1024]{3,2,0,1:T(8,128)(2,1)} %fusion.1, s32[]{:T(128)S(6)} %add.70, s32[]{:T(128)S(6)} %select_n.27), kind=kOutput, calls=%fused_computation.7 | convolution fusion | flops 4294967296 | bytes 29360136 | tf_op jit(solution)/shard_map/fmk,fkn->fmn/dot_general | solution.py:38
  561.5 17.2 %fusion.13 = f32[8,256,1024]{2,1,0:T(8,128)} fusion(f32[8,256,1024]{2,1,0:T(8,128)} %fusion.5, bf16[8,2,1024,1024]{3,2,0,1:T(8,128)(2,1)} %fusion.1, s32[]{:T(128)S(6)} %add.70, s32[]{:T(128)S(6)} %select_n.27), kind=kOutput, calls=%fused_computation.23 | convolution fusion | flops 4297064448 | bytes 37748744 | tf_op jit(solution)/shard_map/fmk,fkn->fmn/dot_general | solution.py:38
  578.7 16.1 %fusion.6 = f32[8,256,1024]{2,1,0:T(8,128)} fusion(bf16[8,2,1024,1024]{3,2,0,1:T(8,128)(2,1)} %fusion.1, f32[8,256,1024]{2,1,0:T(8,128)} %fusion.13), kind=kOutput, calls=%fused_computation.9 | convolution fusion | flops 4297064448 | bytes 33554432 | tf_op jit(solution)/shard_map/fmk,fkn->fmn/dot_general | solution.py:38
  594.8 15.9 %fusion.3 = f32[8,256,1024]{2,1,0:T(8,128)} fusion(bf16[8,2,1024,1024]{3,2,0,1:T(8,128)(2,1)} %fusion.1, f32[8,256,1024]{2,1,0:T(8,128)} %fusion.13), kind=kOutput, calls=%fused_computation.6 | convolution fusion | flops 4297064448 | bytes 33554432 | tf_op jit(solution)/shard_map/fmk,fkn->fmn/dot_general | solution.py:38
  610.7 17.4 %fusion.14 = f32[8,256,1024]{2,1,0:T(8,128)} fusion(f32[8,256,1024]{2,1,0:T(8,128)} %fusion.4, bf16[8,2,1024,1024]{3,2,0,1:T(8,128)(2,1)} %fusion.1, s32[]{:T(128)S(6)} %select_n.27), kind=kOutput, calls=%fused_computation.24 | convolution fusion | flops 4297064448 | bytes 37748740 | tf_op jit(solution)/shard_map/fmk,fkn->fmn/dot_general | solution.py:38
  628.1 16.3 %fusion.2 = f32[8,256,1024]{2,1,0:T(8,128)} fusion(bf16[8,2,1024,1024]{3,2,0,1:T(8,128)(2,1)} %fusion.1, f32[8,256,1024]{2,1,0:T(8,128)} %fusion.14), kind=kOutput, calls=%fused_computation.5 | convolution fusion | flops 4297064448 | bytes 33554432 | tf_op jit(solution)/shard_map/fmk,fkn->fmn/dot_general | solution.py:38
  644.5 28.6 %fusion.11 = (bf16[8,1,256,1024]{3,2,0,1:T(8,128)(2,1)}, bf16[8,1,256,1024]{3,2,0,1:T(8,128)(2,1)}) fusion(f32[8,256,1024]{2,1,0:T(8,128)} %fusion.14, f32[8,256,1024]{2,1,0:T(8,128)} %fusion.13, f32[8]{0:T(128)S(1)} %copy-done.4, f32[8]{0:T(128)S(1)} %copy-done.3, f32[8]{0:T(128)S(1)} %copy-done.6, f32[8]{0:T(128)S(1)} %copy-done.5, ...), kind=kOutput, calls=%fused_computation.19 | convolution fusion | flops 4343201792 | bytes 83886216 | tf_op jit(solution)/shard_map/fmk,fkn->fmn/dot_general | solution.py:38
  673.1 7.6 pad_maximum_fusion
  680.7 8.0 copy.34
  688.7 12.5 %copy.35 = bf16[1,16,256,1024]{2,1,0,3:T(8,128)(2,1)} copy(bf16[1,16,256,1024]{3,2,1,0:T(8,128)(2,1)} %bitcast.73) | data formatting | bytes 16777216 | tf_op jit(solution)/shard_map/convert_element_type | solution.py:85
  701.1 5.6 all-to-all-start.1
  706.8 0.1 copy.38
  706.9 183.5 %all-to-all-done.1 = bf16[1,16,256,1024]{2,1,0,3:T(8,128)(2,1)} async-done(((bf16[1,16,256,1024]{2,1,0,3:T(8,128)(2,1)}), bf16[1,16,256,1024]{2,1,0,3:T(8,128)(2,1)}, u32[]{:S(2)}, u32[]{:S(2)}) %all-to-all-start.1) | async-done | bytes 8388640 | tf_op jit(solution)/shard_map/all_to_all | solution.py:88
  890.4 9.8 %copy.36 = bf16[1,16,256,1024]{2,3,1,0:T(8,128)(2,1)} copy(bf16[1,16,256,1024]{2,1,0,3:T(8,128)(2,1)} %all-to-all-done.1) | data formatting | bytes 16777216 | tf_op jit(solution)/shard_map/all_to_all | solution.py:88
  900.2 11.4 %copy.37 = bf16[8,1,16,256,128]{4,3,2,0,1:T(8,128)(2,1)} copy(bf16[8,1,16,256,128]{3,4,0,2,1:T(8,128)(2,1)} %bitcast.74) | data formatting | bytes 16777216 | tf_op jit(solution)/shard_map/all_to_all | solution.py:88
  911.6 24.2 %convolution_convert_fusion = bf16[256,128,256]{2,1,0:T(8,128)(2,1)} fusion(bf16[128,256,1]{1,0,2:T(8,128)(2,1)S(1)} %reshape.172, bf16[128,256,128]{2,1,0:T(8,128)(2,1)} %bitcast.71), kind=kOutput, calls=%fused_computation.13 | convolution fusion | flops 2155872256 | bytes 25231360 | tf_op jit(solution)/shard_map/csr,ct->srt/dot_general | solution.py:90
  (18 shorter events, 0.1 us)
Async XLA Ops:
  6.5 230.9 %copy-start = (f32[2,64]{1,0:T(2,128)S(1)}, f32[2,64]{1,0:T(2,128)}, u32[]{:S(2)}) copy-start(f32[2,64]{1,0:T(2,128)} %param.3) | copy-start | bytes 1540
  6.5 436.2 %all-gather.2.cloned.1.call-start = ((), (), s32[]{:S(2)}) async-start(), calls=%async_computation.2 | async-start | bytes 41943040 | tf_op jit(solution)/shard_map/all_gather | solution.py:64
  628.1 16.3 %copy-start.3 = (f32[8]{0:T(128)S(1)}, f32[8]{0:T(128)}, u32[]{:S(2)}) copy-start(f32[8]{0:T(128)} %get-tuple-element.11) | copy-start | bytes 100
  628.1 16.3 %copy-start.4 = (f32[8]{0:T(128)S(1)}, f32[8]{0:T(128)}, u32[]{:S(2)}) copy-start(f32[8]{0:T(128)} %get-tuple-element.12) | copy-start | bytes 100
  628.1 16.3 %copy-start.5 = (f32[8]{0:T(128)S(1)}, f32[8]{0:T(128)}, u32[]{:S(2)}) copy-start(f32[8]{0:T(128)} %get-tuple-element.9) | copy-start | bytes 100
  628.1 16.3 %copy-start.6 = (f32[8]{0:T(128)S(1)}, f32[8]{0:T(128)}, u32[]{:S(2)}) copy-start(f32[8]{0:T(128)} %get-tuple-element.10) | copy-start | bytes 100
  701.1 5.7 copy-start.2
  701.1 189.2 %all-to-all-start.1 = ((bf16[1,16,256,1024]{2,1,0,3:T(8,128)(2,1)}), bf16[1,16,256,1024]{2,1,0,3:T(8,128)(2,1)}, u32[]{:S(2)}, u32[]{:S(2)}) async-start(bf16[1,16,256,1024]{2,1,0,3:T(8,128)(2,1)} %copy.35), calls=%async_computation.1 | async-start | bytes 16777216 | tf_op jit(solution)/shard_map/all_to_all | solution.py:88
  911.6 24.3 %copy-start.1 = (f32[2,64]{1,0:T(2,128)S(1)}, f32[2,64]{1,0:T(2,128)}, u32[]{:S(2)}) copy-start(f32[2,64]{1,0:T(2,128)} %param.3) | copy-start | bytes 1540
Sparse Core Ops, SparseCore 0:
  237.6 205.0 all-gather.1
where the time goes:
time: 950 us; the launch traced here: 943 us
  waiting for transfers between devices  388 us (41%)
  blocking collectives  190 us (20%)
  matrix products  177 us (19%)
  local copies, waits for them, and re-layouts  117 us (12%)
  other arithmetic  52 us (5%)
  between operations  13.7 us (1%)
    all_gather x1, waiting for transfers between devices, local(): lax.all_gather(slices, 'src', axis=2, tiled=True).astype(jnp.float32)  204 us
    all_to_all x1, blocking collectives, local(): lax.all_to_all(spectra, 'rcv', split_axis=0, concat_axis=3, tiled=True)  190 us
    all_to_all x1, waiting for transfers between devices, local(): lax.all_to_all(cleaned, 'rcv', split_axis=3, concat_axis=0, tiled=True)  183 us
    dot_general x8, matrix products, multiply(): jnp.einsum('fmk,fkn->fmn', left_side, right_side, preferred_element_type=...  141 us
    convert_element_type x1, local copies, waits for them, and re-layouts, local(): lax.all_gather(slices, 'src', axis=2, tiled=True).astype(jnp.float32)  46.2 us
    convert_element_type x1, other arithmetic, local(): all_rows = (0.5 * (whole + jnp.swapaxes(whole, 2, 3))).astype(jnp.bfloat16)  42.8 us
    dot_general x1, matrix products, local(): jnp.einsum('csr,ct->srt', returned, inverse, preferred_element_type=jnp.f...  24.2 us
    all_to_all x2, local copies, waits for them, and re-layouts, local(): lax.all_to_all(cleaned, 'rcv', split_axis=3, concat_axis=0, tiled=True)  21.2 us
  transfers between devices with their start and end apart: 2, of which 2 were waited for; matrix products, arithmetic and copies ran while one was open for 0% of the time, Pallas kernels for 0%

commit v1 on v0

--- a/solution.py
+++ b/solution.py
@@ -58,7 +58,15 @@
         "ct,srt->csr", forward, wavefield, preferred_element_type=jnp.float32
     ).astype(jnp.bfloat16)
     spectra = spectra.reshape(groups, 2 * per_dev, src_rows, rcv_cols)
-    slices = lax.all_to_all(spectra, "rcv", split_axis=0, concat_axis=3, tiled=True)
+    ways, here = (lax.axis_size("rcv"), lax.axis_index("rcv"))
+    width = spectra.shape[0] // ways
+    turned = jnp.roll(spectra, -here * width, axis=0)
+    got = [lax.slice_in_dim(turned, 0, width, axis=0)]
+    for far in range(1, ways):
+        sent = lax.slice_in_dim(turned, far * width, (far + 1) * width, axis=0)
+        got.append(lax.ppermute(sent, "rcv", [(d, (d + far) % ways) for d in range(ways)]))
+    line = jnp.concatenate(got[::-1], axis=3)
+    slices = jnp.roll(line, (here + 1) * got[0].shape[3], axis=3)
     total_cols = slices.shape[3]
     slices = slices.reshape(per_dev, 2, src_rows, total_cols)
     whole = lax.all_gather(slices, "src", axis=2, tiled=True).astype(jnp.float32)

time: 950 us -> 996 us (1.048)
  blocking collectives: 190 us -> 0 us
  waiting for transfers between devices: 388 us -> 559 us
  local copies, waits for them, and re-layouts: 117 us -> 155 us
    all_to_all x1 -> x0, blocking collectives: 190 us -> none  [local(): lax.all_to_all(spectra, 'rcv', split_axis=0, concat_axis=3, tiled=True)]
    ppermute x0 -> x7, waiting for transfers between devices: none -> 173 us  [local(): lax.ppermute(sent, 'rcv', [(d, (d + far) % ways) for d in range(ways)])]
    unnamed x14 -> x31, local copies, waits for them, and re-layouts: 0.03 us -> 30.2 us
  transfers between devices with their start and end apart: 2 -> 9, of which waited for: 2 -> 6; matrix products, arithmetic and copies ran while one was open for 0% -> 1% of each run, Pallas kernels for 0% -> 0%
where the time goes in v1:
time: 996 us; the launch traced here: 986 us
  waiting for transfers between devices  559 us (56%)
  matrix products  185 us (19%)
  local copies, waits for them, and re-layouts  155 us (16%)
  other arithmetic  57.5 us (6%)
  starting transfers between devices  15.4 us (2%)
  between operations  14 us (1%)
    all_gather x1, waiting for transfers between devices, local(): lax.all_gather(slices, 'src', axis=2, tiled=True).astype(jnp.float32)  202 us
    all_to_all x1, waiting for transfers between devices, local(): lax.all_to_all(cleaned, 'rcv', split_axis=3, concat_axis=0, tiled=True)  183 us
    ppermute x7, waiting for transfers between devices, local(): lax.ppermute(sent, 'rcv', [(d, (d + far) % ways) for d in range(ways)])  173 us
    dot_general x8, matrix products, multiply(): jnp.einsum('fmk,fkn->fmn', left_side, right_side, preferred_element_type=...  150 us
    convert_element_type x1, local copies, waits for them, and re-layouts, local(): lax.all_gather(slices, 'src', axis=2, tiled=True).astype(jnp.float32)  46.3 us
    convert_element_type x1, other arithmetic, local(): all_rows = (0.5 * (whole + jnp.swapaxes(whole, 2, 3))).astype(jnp.bfloat16)  42.7 us
    unnamed x31, local copies, waits for them, and re-layouts  30.2 us
    dot_general x1, matrix products, local(): jnp.einsum('csr,ct->srt', returned, inverse, preferred_element_type=jnp.f...  24.3 us
  transfers between devices with their start and end apart: 9, of which 6 were waited for; matrix products, arithmetic and copies ran while one was open for 1% of the time, Pallas kernels for 0%

profile of v1, /device:TPU:0, one launch (start us, length us, event | category | flops | bytes accessed | tf_op | source)
XLA Modules:
  0.0 985.9 jit_solution(1199431623306373723)
XLA Ops:
  7.6 11.1 %convolution_convert_fusion.1 = bf16[128,256,128]{2,0,1:T(8,128)(2,1)} fusion(bf16[128,256,1]{1,0,2:T(8,128)(2,1)S(1)} %reshape.170, bf16[256,128,256]{2,1,0:T(8,128)(2,1)} %param.2), kind=kOutput, calls=%fused_computation.21 | convolution fusion | flops 2151677952 | bytes 25231360 | tf_op jit(solution)/shard_map/ct,srt->csr/dot_general | solution.py:57
  18.8 12.0 %copy.31 = bf16[8,16,256,128]{3,2,1,0:T(8,128)(2,1)} copy(bf16[8,16,256,128]{3,1,0,2:T(8,128)(2,1)} %bitcast.66) | data formatting | bytes 16777216 | tf_op jit(solution)/shard_map/reshape | solution.py:60
  30.8 5.6 fusion.10
  36.5 3.3 copy-done.2
  39.7 2.4 fusion.31
  42.1 6.0 collective-permute-start
  48.6 3.0 collective-permute-start.3
  51.6 20.1 %collective-permute-done = bf16[1,16,256,128]{3,2,1,0:T(8,128)(2,1)S(1)} collective-permute-done((bf16[1,16,256,128]{3,2,1,0:T(8,128)(2,1)S(1)}, bf16[1,16,256,128]{3,2,1,0:T(8,128)(2,1)S(1)}, u32[]{:S(2)}, u32[]{:S(2)}) %collective-permute-start) | collective-permute-done | bytes 1048608 | tf_op jit(solution)/shard_map/ppermute | solution.py:67
  71.7 22.5 %collective-permute-done.1 = bf16[1,16,256,128]{3,2,1,0:T(8,128)(2,1)S(1)} collective-permute-done((bf16[1,16,256,128]{3,2,1,0:T(8,128)(2,1)S(1)}, bf16[1,16,256,128]{3,2,1,0:T(8,128)(2,1)S(1)}, u32[]{:S(2)}, u32[]{:S(2)}) %collective-permute-start.1) | collective-permute-done | bytes 1048608 | tf_op jit(solution)/shard_map/ppermute | solution.py:67
  96.6 20.3 %collective-permute-done.2 = bf16[1,16,256,128]{3,2,1,0:T(8,128)(2,1)S(1)} collective-permute-done((bf16[1,16,256,128]{3,2,1,0:T(8,128)(2,1)}, bf16[1,16,256,128]{3,2,1,0:T(8,128)(2,1)S(1)}, u32[]{:S(2)}, u32[]{:S(2)}) %collective-permute-start.2) | collective-permute-done | bytes 1048608 | tf_op jit(solution)/shard_map/ppermute | solution.py:67
  117.9 110.0 %collective-permute-done.3 = bf16[1,16,256,128]{3,2,1,0:T(8,128)(2,1)} collective-permute-done((bf16[1,16,256,128]{3,2,1,0:T(8,128)(2,1)}, bf16[1,16,256,128]{3,2,1,0:T(8,128)(2,1)}, u32[]{:S(2)}, u32[]{:S(2)}) %collective-permute-start.3) | collective-permute-done | bytes 1048608 | tf_op jit(solution)/shard_map/ppermute | solution.py:67
  253.9 8.0 constant_dynamic-slice_fusion.1
  261.9 11.7 %copy.33 = bf16[8,2,256,1024]{2,3,0,1:T(8,128)(2,1)} copy(bf16[8,2,256,1024]{3,2,1,0:T(8,128)(2,1)} %bitcast.68) | data formatting | bytes 16777216 | tf_op jit(solution)/shard_map/reshape | solution.py:71
  274.9 202.1 %all-gather.2.cloned.1.call-done = bf16[8,2,1024,1024]{2,3,0,1:T(8,128)(2,1)} async-done(((bf16[8,2,256,1024]{2,3,0,1:T(8,128)(2,1)}), bf16[8,2,1024,1024]{2,3,0,1:T(8,128)(2,1)}) %all-gather.2.cloned.1.call-update) | async-done | bytes 33554448 | tf_op jit(solution)/shard_map/all_gather | solution.py:72
  477.0 46.3 %copy.34 = f32[8,2,1024,1024]{3,2,0,1:T(8,128)} copy(bf16[8,2,1024,1024]{2,3,0,1:T(8,128)(2,1)} %all-gather.2.cloned.1.call-done) | data formatting | bytes 100663296 | tf_op jit(solution)/shard_map/convert_element_type | solution.py:72
  523.3 42.7 %fusion.1 = bf16[8,2,1024,1024]{3,2,0,1:T(8,128)(2,1)} fusion(f32[8,2,1024,1024]{3,2,0,1:T(8,128)} %copy.34, bf16[8,2,1024,1024]{2,3,0,1:T(8,128)(2,1)} %all-gather.2.cloned.1.call-done), kind=kLoop, calls=%fused_computation.2 | loop fusion | flops 67108864 | bytes 134217728 | tf_op jit(solution)/shard_map/convert_element_type | solution.py:73
  566.0 14.8 %fusion.5 = f32[8,256,1024]{2,1,0:T(8,128)} fusion(bf16[8,2,1024,1024]{3,2,0,1:T(8,128)(2,1)} %fusion.1, s32[]{:T(128)S(6)} %select_n.53), kind=kOutput, calls=%fused_computation.10 | convolution fusion | flops 4294967296 | bytes 29360132 | tf_op jit(solution)/shard_map/fmk,fkn->fmn/dot_general | solution.py:38
  580.8 15.0 %fusion.4 = f32[8,256,1024]{2,1,0:T(8,128)} fusion(bf16[8,2,1024,1024]{3,2,0,1:T(8,128)(2,1)} %fusion.1, s32[]{:T(128)S(6)} %add.97, s32[]{:T(128)S(6)} %select_n.53), kind=kOutput, calls=%fused_computation.9 | convolution fusion | flops 4294967296 | bytes 29360136 | tf_op jit(solution)/shard_map/fmk,fkn->fmn/dot_general | solution.py:38
  595.8 17.2 %fusion.14 = f32[8,256,1024]{2,1,0:T(8,128)} fusion(f32[8,256,1024]{2,1,0:T(8,128)} %fusion.5, bf16[8,2,1024,1024]{3,2,0,1:T(8,128)(2,1)} %fusion.1, s32[]{:T(128)S(6)} %add.97, s32[]{:T(128)S(6)} %select_n.53), kind=kOutput, calls=%fused_computation.26 | convolution fusion | flops 4297064448 | bytes 37748744 | tf_op jit(solution)/shard_map/fmk,fkn->fmn/dot_general | solution.py:38
  613.0 24.7 %fusion.6 = f32[8,256,1024]{2,1,0:T(8,128)} fusion(bf16[8,2,1024,1024]{3,2,0,1:T(8,128)(2,1)} %fusion.1, f32[8,256,1024]{2,1,0:T(8,128)} %fusion.14), kind=kOutput, calls=%fused_computation.11 | convolution fusion | flops 4297064448 | bytes 33554432 | tf_op jit(solution)/shard_map/fmk,fkn->fmn/dot_general | solution.py:38
  637.7 15.9 %fusion.3 = f32[8,256,1024]{2,1,0:T(8,128)} fusion(bf16[8,2,1024,1024]{3,2,0,1:T(8,128)(2,1)} %fusion.1, f32[8,256,1024]{2,1,0:T(8,128)} %fusion.14), kind=kOutput, calls=%fused_computation.8 | convolution fusion | flops 4297064448 | bytes 33554432 | tf_op jit(solution)/shard_map/fmk,fkn->fmn/dot_general | solution.py:38
  653.6 17.4 %fusion.15 = f32[8,256,1024]{2,1,0:T(8,128)} fusion(f32[8,256,1024]{2,1,0:T(8,128)} %fusion.4, bf16[8,2,1024,1024]{3,2,0,1:T(8,128)(2,1)} %fusion.1, s32[]{:T(128)S(6)} %select_n.53), kind=kOutput, calls=%fused_computation.27 | convolution fusion | flops 4297064448 | bytes 37748740 | tf_op jit(solution)/shard_map/fmk,fkn->fmn/dot_general | solution.py:38
  671.0 16.1 %fusion.2 = f32[8,256,1024]{2,1,0:T(8,128)} fusion(bf16[8,2,1024,1024]{3,2,0,1:T(8,128)(2,1)} %fusion.1, f32[8,256,1024]{2,1,0:T(8,128)} %fusion.15), kind=kOutput, calls=%fused_computation.7 | convolution fusion | flops 4297064448 | bytes 33554432 | tf_op jit(solution)/shard_map/fmk,fkn->fmn/dot_general | solution.py:38
  687.2 28.6 %fusion.12 = (bf16[8,1,256,1024]{3,2,0,1:T(8,128)(2,1)}, bf16[8,1,256,1024]{3,2,0,1:T(8,128)(2,1)}) fusion(f32[8,256,1024]{2,1,0:T(8,128)} %fusion.15, f32[8,256,1024]{2,1,0:T(8,128)} %fusion.14, f32[8]{0:T(128)S(1)} %copy-done.5, f32[8]{0:T(128)S(1)} %copy-done.4, f32[8]{0:T(128)S(1)} %copy-done.7, f32[8]{0:T(128)S(1)} %copy-done.6, ...), kind=kOutput, calls=%fused_computation.22 | convolution fusion | flops 4343201792 | bytes 83886216 | tf_op jit(solution)/shard_map/fmk,fkn->fmn/dot_general | solution.py:38
  715.8 7.6 pad_maximum_fusion
  723.4 8.0 copy.35
  731.4 12.5 %copy.36 = bf16[1,16,256,1024]{2,1,0,3:T(8,128)(2,1)} copy(bf16[1,16,256,1024]{3,2,1,0:T(8,128)(2,1)} %bitcast.69) | data formatting | bytes 16777216 | tf_op jit(solution)/shard_map/convert_element_type | solution.py:93
  743.9 5.6 all-to-all-start
  749.6 183.5 %all-to-all-done = bf16[1,16,256,1024]{2,1,0,3:T(8,128)(2,1)} async-done(((bf16[1,16,256,1024]{2,1,0,3:T(8,128)(2,1)}), bf16[1,16,256,1024]{2,1,0,3:T(8,128)(2,1)}, u32[]{:S(2)}, u32[]{:S(2)}) %all-to-all-start) | async-done | bytes 8388640 | tf_op jit(solution)/shard_map/all_to_all | solution.py:96
  933.1 9.8 copy.37
  942.9 11.4 %copy.38 = bf16[8,1,16,256,128]{4,3,2,0,1:T(8,128)(2,1)} copy(bf16[8,1,16,256,128]{3,4,0,2,1:T(8,128)(2,1)} %bitcast.70) | data formatting | bytes 16777216 | tf_op jit(solution)/shard_map/all_to_all | solution.py:96
  954.3 24.3 %convolution_convert_fusion = bf16[256,128,256]{2,1,0:T(8,128)(2,1)} fusion(bf16[128,256,1]{1,0,2:T(8,128)(2,1)S(1)} %reshape.171, bf16[128,256,128]{2,1,0:T(8,128)(2,1)} %bitcast.67), kind=kOutput, calls=%fused_computation.15 | convolution fusion | flops 2155872256 | bytes 25231360 | tf_op jit(solution)/shard_map/csr,ct->srt/dot_general | solution.py:98
  (51 shorter events, 32.4 us)
Async XLA Ops:
  6.5 267.1 %copy-start = (f32[2,64]{1,0:T(2,128)S(1)}, f32[2,64]{1,0:T(2,128)}, u32[]{:S(2)}) copy-start(f32[2,64]{1,0:T(2,128)} %param.3) | copy-start | bytes 1540
  6.5 470.5 %all-gather.2.cloned.1.call-start = ((), (), s32[]{:S(2)}) async-start(), calls=%async_computation.1 | async-start | bytes 41943040 | tf_op jit(solution)/shard_map/all_gather | solution.py:72
  36.5 3.3 copy-start.2
  42.1 29.6 %collective-permute-start = (bf16[1,16,256,128]{3,2,1,0:T(8,128)(2,1)S(1)}, bf16[1,16,256,128]{3,2,1,0:T(8,128)(2,1)S(1)}, u32[]{:S(2)}, u32[]{:S(2)}) collective-permute-start(bf16[1,16,256,128]{3,2,1,0:T(8,128)(2,1)S(1)} %get-tuple-element.13), channel_id=1, source_target_pairs={{0,7},{1,0},{2,1},{3,2},{4,3},{5,4},{6,5},{7,6},{8,15},{9,8},{10,9... | collective-permute-start | bytes 3145736 | tf_op jit(solution)/shard_map/ppermute | solution.py:67
  48.1 46.1 %collective-permute-start.1 = (bf16[1,16,256,128]{3,2,1,0:T(8,128)(2,1)S(1)}, bf16[1,16,256,128]{3,2,1,0:T(8,128)(2,1)S(1)}, u32[]{:S(2)}, u32[]{:S(2)}) collective-permute-start(bf16[1,16,256,128]{3,2,1,0:T(8,128)(2,1)S(1)} %get-tuple-element.12), channel_id=1, source_target_pairs={{0,6},{1,7},{2,0},{3,1},{4,2},{5,3},{6,4},{7,5},{8,14},{9,15},{10,... | collective-permute-start | bytes 3145736 | tf_op jit(solution)/shard_map/ppermute | solution.py:67
  48.6 68.2 %collective-permute-start.2 = (bf16[1,16,256,128]{3,2,1,0:T(8,128)(2,1)}, bf16[1,16,256,128]{3,2,1,0:T(8,128)(2,1)S(1)}, u32[]{:S(2)}, u32[]{:S(2)}) collective-permute-start(bf16[1,16,256,128]{3,2,1,0:T(8,128)(2,1)} %get-tuple-element.11), channel_id=1, source_target_pairs={{0,5},{1,6},{2,7},{3,0},{4,1},{5,2},{6,3},{7,4},{8,13},{9,14},{10,... | collective-permute-start | bytes 3145736 | tf_op jit(solution)/shard_map/ppermute | solution.py:67
  48.6 179.3 %collective-permute-start.3 = (bf16[1,16,256,128]{3,2,1,0:T(8,128)(2,1)}, bf16[1,16,256,128]{3,2,1,0:T(8,128)(2,1)}, u32[]{:S(2)}, u32[]{:S(2)}) collective-permute-start(bf16[1,16,256,128]{3,2,1,0:T(8,128)(2,1)} %get-tuple-element.10), channel_id=1, source_target_pairs={{0,4},{1,5},{2,6},{3,7},{4,0},{5,1},{6,2},{7,3},{8,12},{9,13},{10,... | collective-permute-start | bytes 3145736 | tf_op jit(solution)/shard_map/ppermute | solution.py:67
  51.6 178.6 %collective-permute-start.4 = (bf16[1,16,256,128]{3,2,1,0:T(8,128)(2,1)}, bf16[1,16,256,128]{3,2,1,0:T(8,128)(2,1)}, u32[]{:S(2)}, u32[]{:S(2)}) collective-permute-start(bf16[1,16,256,128]{3,2,1,0:T(8,128)(2,1)} %get-tuple-element.9), channel_id=1, source_target_pairs={{0,3},{1,4},{2,5},{3,6},{4,7},{5,0},{6,1},{7,2},{8,11},{9,12},{10,... | collective-permute-start | bytes 3145736 | tf_op jit(solution)/shard_map/ppermute | solution.py:67
  71.7 160.7 %collective-permute-start.5 = (bf16[1,16,256,128]{3,2,1,0:T(8,128)(2,1)}, bf16[1,16,256,128]{3,2,1,0:T(8,128)(2,1)}, u32[]{:S(2)}, u32[]{:S(2)}) collective-permute-start(bf16[1,16,256,128]{3,2,1,0:T(8,128)(2,1)} %get-tuple-element.8), channel_id=1, source_target_pairs={{0,2},{1,3},{2,4},{3,5},{4,6},{5,7},{6,0},{7,1},{8,10},{9,11},{10,... | collective-permute-start | bytes 3145736 | tf_op jit(solution)/shard_map/ppermute | solution.py:67
  94.2 140.6 %collective-permute-start.6 = (bf16[1,16,256,128]{3,2,1,0:T(8,128)(2,1)}, bf16[1,16,256,128]{3,2,1,0:T(8,128)(2,1)}, u32[]{:S(2)}, u32[]{:S(2)}) collective-permute-start(bf16[1,16,256,128]{3,2,1,0:T(8,128)(2,1)} %get-tuple-element.7), channel_id=1, source_target_pairs={{0,1},{1,2},{2,3},{3,4},{4,5},{5,6},{6,7},{7,0},{8,9},{9,10},{10,1... | collective-permute-start | bytes 3145736 | tf_op jit(solution)/shard_map/ppermute | solution.py:67
  671.0 16.1 %copy-start.4 = (f32[8]{0:T(128)S(1)}, f32[8]{0:T(128)}, u32[]{:S(2)}) copy-start(f32[8]{0:T(128)} %get-tuple-element.18) | copy-start | bytes 100
  671.0 16.1 %copy-start.5 = (f32[8]{0:T(128)S(1)}, f32[8]{0:T(128)}, u32[]{:S(2)}) copy-start(f32[8]{0:T(128)} %get-tuple-element.19) | copy-start | bytes 100
  671.0 16.1 %copy-start.6 = (f32[8]{0:T(128)S(1)}, f32[8]{0:T(128)}, u32[]{:S(2)}) copy-start(f32[8]{0:T(128)} %get-tuple-element.16) | copy-start | bytes 100
  671.0 16.1 %copy-start.7 = (f32[8]{0:T(128)S(1)}, f32[8]{0:T(128)}, u32[]{:S(2)}) copy-start(f32[8]{0:T(128)} %get-tuple-element.17) | copy-start | bytes 100
  743.9 5.7 copy-start.3
  743.9 189.2 %all-to-all-start = ((bf16[1,16,256,1024]{2,1,0,3:T(8,128)(2,1)}), bf16[1,16,256,1024]{2,1,0,3:T(8,128)(2,1)}, u32[]{:S(2)}, u32[]{:S(2)}) async-start(bf16[1,16,256,1024]{2,1,0,3:T(8,128)(2,1)} %copy.36), calls=%async_computation | async-start | bytes 16777216 | tf_op jit(solution)/shard_map/all_to_all | solution.py:96
  954.3 24.3 %copy-start.1 = (f32[2,64]{1,0:T(2,128)S(1)}, f32[2,64]{1,0:T(2,128)}, u32[]{:S(2)}) copy-start(f32[2,64]{1,0:T(2,128)} %param.3) | copy-start | bytes 1540
Sparse Core Ops, SparseCore 0:
  273.8 203.2 all-gather.1
